TPU v7x, 768 devices: a whole 4x8x12 slice. The times are simulated.
768 devices in a mesh: row: 32 (over z_hi, y, core), col: 24 (over z_lo, x).
Axes of the slice: x: 4, y: 8, z: 12 (z_hi: 2, z_lo: 6; z = z_hi * 6 + z_lo), core: 2. Of those that a mesh axis runs over, the one named last changes fastest.
Arguments:
- left_factors: bfloat16 [1536, 32, 512], P('col', None, 'row'), may hold values from -0.15625 to 0.15625
- right_factors: bfloat16 [1536, 4, 512], P('col'), may hold values from -0.15625 to 0.15625
- amplitudes: bfloat16 [1536, 512, 512], P('col', 'row'), may hold values from -0.46875 to 0.46875
Outputs:
- ladder: float32 [1536, 32, 4], P('col', 'row')
All inputs are finite; a program needn't handle non-finite values.
Results may differ from a plain program's by a relative error of at most 0.0029.
Values may be sent and summed in bfloat16 or wider, within the bound.
No kernel may reach another device: no remote copies, remote signals or barrier semaphores. Data moves between devices by JAX's collectives and lax.ppermute only.
A program may use at most 64 MiB of HBM per device.

v0:
```python
import jax
import jax.numpy as jnp
from jax import lax
from jax.sharding import PartitionSpec as P


def joined_along(tiles, dim):
    shape = list(tiles.shape[1:])
    shape[dim] *= tiles.shape[0]
    return jnp.moveaxis(tiles, 0, dim).reshape(shape)


def copy_for_each(x, axis):
    peers = lax.axis_size(axis)
    return lax.all_to_all(jnp.broadcast_to(x[None], (peers, *x.shape)), axis, 0, 0, tiled=True)


def gathered_copies(x, axis, dim):
    return joined_along(copy_for_each(x, axis), dim)


def cut_along(x, dim, peers):
    before, after = (x.shape[:dim], x.shape[dim + 1 :])
    return jnp.moveaxis(x.reshape(*before, peers, -1, *after), dim, 0)


def sum_at_owner(x, axis, dim):
    tiles = cut_along(x, dim, lax.axis_size(axis))
    arrived = lax.all_to_all(tiles, axis, split_axis=0, concat_axis=0, tiled=True)
    return arrived.sum(axis=0)


def contract_aux(left_part, right_part):
    return lax.dot_general(
        left_part, right_part, (((0,), (0,)), ((), ())), preferred_element_type=jnp.float32
    )


def per_device(left_factors, right_factors, amplitudes):
    count_a = left_factors.shape[1]
    c_block = left_factors.shape[2]
    count_b = right_factors.shape[1]
    width = right_factors.shape[2]
    pairs = amplitudes.shape[0]
    left_full = gathered_copies(left_factors, "col", 0)
    left_flat = left_full.reshape(left_full.shape[0], count_a * c_block)
    right_full = lax.all_gather(right_factors, "col", axis=0, tiled=True)
    tile = contract_aux(left_flat, right_full.reshape(right_full.shape[0], count_b * width))
    rounded = tile.astype(jnp.bfloat16).reshape(count_a, c_block, count_b, width)
    matrix = jnp.transpose(rounded, (1, 3, 0, 2)).reshape(c_block * width, count_a * count_b)
    flat_amps = amplitudes.reshape(pairs, c_block * width)
    partial_value = jnp.dot(flat_amps, matrix, preferred_element_type=jnp.float32)
    partial_value = partial_value.reshape(pairs, count_a, count_b)
    return sum_at_owner(partial_value, "row", 1)


def solution(mesh):
    placed = (P("col", None, "row"), P("col", None, None), P("col", "row", None))
    return jax.shard_map(
        per_device, mesh=mesh, in_specs=placed, out_specs=P("col", "row", None), check_vma=False
    )
```

profile of v0, /device:TPU:1, one launch (start us, length us, event | category | flops | bytes accessed | tf_op | source)
XLA Modules:
  0.0 238.3 jit_solution(17014378399224854807)
XLA Ops:
  6.5 0.0 copy-start
  6.5 0.0 all-gather.2.cloned.1.call-start
  6.5 0.7 all-gather.2.cloned.1.call-update
  7.3 0.2 copy-done
  7.4 0.7 broadcast_bitcast_fusion
  8.1 3.3 %reshape.18 = bf16[24,2,16384]{2,1,0:T(2,128)(2,1)} reshape(bf16[24,32,16,64]{3,2,1,0:T(8,128)(2,1)S(1)} %broadcast_bitcast_fusion) | data formatting | bytes 3145728
  11.4 0.0 copy-start.2
  11.4 15.6 %all-to-all-start = ((bf16[24,2,16384]{2,1,0:T(2,128)(2,1)}), bf16[24,2,16384]{2,1,0:T(2,128)(2,1)}, u32[]{:S(2)}, u32[]{:S(2)}) async-start(bf16[24,2,16384]{2,1,0:T(2,128)(2,1)} %reshape.18), calls=%async_computation | async-start | bytes 3145728 | tf_op jit(solution)/shard_map/all_to_all | solution.py:15
  27.0 0.0 copy-done.2
  27.0 1.6 copy.13
  28.6 72.9 %all-to-all-done = bf16[24,2,16384]{2,1,0:T(2,128)(2,1)} async-done(((bf16[24,2,16384]{2,1,0:T(2,128)(2,1)}), bf16[24,2,16384]{2,1,0:T(2,128)(2,1)}, u32[]{:S(2)}, u32[]{:S(2)}) %all-to-all-start) | async-done | bytes 1572896 | tf_op jit(solution)/shard_map/all_to_all | solution.py:15
  101.5 5.2 %reshape.19 = bf16[24,32,16,64]{3,2,1,0:T(8,128)(2,1)S(1)} reshape(bf16[24,2,16384]{2,1,0:T(2,128)(2,1)} %all-to-all-done) | data formatting | bytes 3145728
  106.6 5.3 %copy.7 = bf16[24,64,32,16]{1,0,3,2:T(8,128)(2,1)} copy(bf16[24,64,32,16]{1,3,2,0:T(8,128)(2,1)S(1)} %bitcast.32) | data formatting | bytes 3145728 | tf_op jit(solution)/shard_map/all_to_all | solution.py:15
  112.0 4.4 %reshape_reshape.6 = bf16[1536,512]{0,1:T(8,128)(2,1)S(1)} reshape(bf16[24,64,32,16]{1,0,3,2:T(8,128)(2,1)} %copy.7) | data formatting | bytes 3145728 | tf_op jit(solution)/shard_map/reshape;reshape | solution.py:46
  116.4 56.9 %all-gather.2.cloned.1.call-done = bf16[1536,4,512]{2,1,0:T(4,128)(2,1)} async-done(((bf16[64,4,512]{2,1,0:T(4,128)(2,1)}), bf16[1536,4,512]{2,1,0:T(4,128)(2,1)}) %all-gather.2.cloned.1.call-update) | async-done | bytes 6291472 | tf_op jit(solution)/shard_map/all_gather | solution.py:47
  173.3 5.5 %copy.11 = bf16[192,8,4,512]{3,1,2,0:T(8,128)(2,1)S(1)} copy(bf16[192,8,4,512]{3,2,1,0:T(4,128)(2,1)} %bitcast.35) | data formatting | bytes 12582912
  178.8 4.6 %convolution_convert_fusion = bf16[512,2048]{1,0:T(8,128)(2,1)} fusion(bf16[1536,512]{0,1:T(8,128)(2,1)S(1)} %reshape_reshape.6, bf16[1536,2048]{1,0:T(8,128)(2,1)S(1)} %bitcast.36), kind=kOutput, calls=%fused_computation | convolution fusion | flops 3222274048 | bytes 9961472 | tf_op jit(solution)/shard_map/dot_general | solution.py:34
  183.4 3.5 %reshape.15 = bf16[32,16,4,512]{3,2,1,0:T(4,128)(2,1)S(1)} reshape(bf16[512,2048]{1,0:T(8,128)(2,1)} %convolution_convert_fusion) | data formatting | bytes 4194304 | tf_op jit(solution)/shard_map/reshape | solution.py:49
  186.9 0.6 copy.8
  187.5 0.0 copy-start.1
  187.5 1.4 copy.12
  188.9 0.0 copy-done.1
  189.0 0.8 convolution_bitcast_fusion
  189.8 0.1 copy.9
  189.9 0.1 reshape.20
  190.0 39.5 %all_to_all.10 = f32[32,1,256]{2,1,0:T(1,128)S(1)} all-to-all(f32[32,1,256]{2,1,0:T(1,128)S(1)} %reshape.20), channel_id=1, replica_groups=mesh['row'=32,'col'=24] {'row'}, dimensions={0} | all-to-all | bytes 65536 | tf_op jit(solution)/shard_map/all_to_all | solution.py:29
  229.5 0.5 broadcast.1
  230.0 0.7 reduce.1
  230.7 0.1 reshape.21
  230.8 0.6 bitcast_reduce_fusion
Async XLA Ops:
  6.5 0.9 copy-start
  6.5 166.7 %all-gather.2.cloned.1.call-start = ((), (), s32[]{:S(2)}) async-start(), calls=%async_computation.2 | async-start | bytes 6553600 | tf_op jit(solution)/shard_map/all_gather | solution.py:47
  11.4 15.6 %copy-start.2 = (bf16[64,16,512]{2,1,0:T(8,128)(2,1)S(1)}, bf16[64,16,512]{2,1,0:T(8,128)(2,1)}, u32[]{:S(2)}) copy-start(bf16[64,16,512]{2,1,0:T(8,128)(2,1)} %param.5) | copy-start | bytes 3145732
  11.4 90.1 %all-to-all-start = ((bf16[24,2,16384]{2,1,0:T(2,128)(2,1)}), bf16[24,2,16384]{2,1,0:T(2,128)(2,1)}, u32[]{:S(2)}, u32[]{:S(2)}) async-start(bf16[24,2,16384]{2,1,0:T(2,128)(2,1)} %reshape.18), calls=%async_computation | async-start | bytes 3145728 | tf_op jit(solution)/shard_map/all_to_all | solution.py:15
  187.5 1.4 copy-start.1
Sparse Core Ops, SparseCore 0:
  9.7 163.5 all-gather.1
where the time goes:
time: 239 us; the launch traced here: 238 us
  waiting for transfers between devices  130 us (54%)
  blocking collectives  39.5 us (17%)
  local copies, waits for them, and re-layouts  32.4 us (14%)
  starting transfers between devices  15.6 us (7%)
  between operations  13.5 us (6%)
  matrix products  5.48 us (2%)
    all_to_all x1, waiting for transfers between devices, copy_for_each(): lax.all_to_all(jnp.broadcast_to(x[None], (peers, *x.shape)), axis, 0, 0,...  72.9 us
    all_gather x1, waiting for transfers between devices, per_device(): right_full = lax.all_gather(right_factors, 'col', axis=0, tiled=True)  56.9 us
    all_to_all x1, blocking collectives, sum_at_owner(): lax.all_to_all(tiles, axis, split_axis=0, concat_axis=0, tiled=True)  39.5 us
    unnamed x14, local copies, waits for them, and re-layouts  18 us
    all_to_all x1, starting transfers between devices, copy_for_each(): lax.all_to_all(jnp.broadcast_to(x[None], (peers, *x.shape)), axis, 0, 0,...  15.6 us
    all_to_all x1, local copies, waits for them, and re-layouts, copy_for_each(): lax.all_to_all(jnp.broadcast_to(x[None], (peers, *x.shape)), axis, 0, 0,...  5.35 us
  transfers between devices with their start and end apart: 2, of which 2 were waited for; matrix products, arithmetic and copies ran while one was open for 9% of the time, Pallas kernels for 0%

commit v1 on v0

v1 whole, which is shorter than its diff:
```python
import jax
import jax.numpy as jnp
from jax import lax
from jax.experimental import pallas as pl
from jax.experimental.pallas import tpu as pltpu
from jax.sharding import Mesh, PartitionSpec as P


LANES = 128
ZH, YN, CORES, ZN, XN = 2, 8, 2, 6, 4
ZHY = ZH * YN
XC, XD = 2, 2
HALF = 32
C_PART, D_PART = 8, 256
SLOTS = 4
KERNEL_VMEM = 60 * 1024 * 1024


def exchange(x, axis):
    return lax.all_to_all(x, axis, 0, 0, tiled=True)


def ladder_kernel(where_ref, *refs):
    hbm, out_ref, (left_ref, right_ref, amps_ref, sems) = refs[:13], refs[13], refs[14:]
    core, y, x = where_ref[0], where_ref[1], where_ref[2]
    targets = [left_ref] + [right_ref.at[i] for i in range(2 * SLOTS)] + [amps_ref.at[s] for s in range(XN)]
    copies = [pltpu.make_async_copy(a, b, sems.at[i]) for i, (a, b) in enumerate(zip(hbm, targets))]
    for copy in copies:
        copy.start()

    def left_of(half):
        start = pl.multiple_of(half * HALF, HALF)
        parts = [left_ref[i, z, pl.ds(start, HALF), :] for z in range(ZN) for i in range(XN)]
        return jnp.concatenate(parts, axis=0)

    def right_of(who):
        cols = []
        for slot in range(SLOTS):
            for t in range(2):
                rows = [right_ref[who * SLOTS + slot, k, t] for k in range(ZN * XN)]
                cols.append(jnp.concatenate(rows, axis=0))
        return jnp.concatenate(cols, axis=1)

    dims = (((0,), (0,)), ((), ()))
    for copy in copies[: 1 + SLOTS]:
        copy.wait()
    ints = lax.dot_general(left_of(core), right_of(0), dims, preferred_element_type=jnp.float32)
    for copy in copies[1 + SLOTS : 1 + 2 * SLOTS]:
        copy.wait()
    ints = ints + lax.dot_general(left_of(1 - core), right_of(1), dims, preferred_element_type=jnp.float32)
    ints = ints.astype(jnp.bfloat16)
    for copy in copies[1 + 2 * SLOTS :]:
        copy.wait()
    acc = jnp.zeros((LANES, 256), jnp.float32)
    for c in range(C_PART):
        rhs = jnp.concatenate(
            [ints[c * 32 : c * 32 + 32, i * D_PART : (i + 1) * D_PART] for i in range(SLOTS)], axis=0
        )
        amps = jnp.concatenate([amps_ref[s, c] for s in range(XN)], axis=0)
        acc = acc + lax.dot_general(rhs, amps, (((1,), (1,)), ((), ())), preferred_element_type=jnp.float32)
    for slot in range(SLOTS):
        row = pl.multiple_of(lax.rem(y + slot, SLOTS) * YN, YN)
        for s in range(XN):
            to = lax.rem(x + XN - s, XN)
            for k in range(CORES):
                r = slot * 32 + k * 16
                both = [acc[r + h * YN : r + h * YN + YN, s * 64 : s * 64 + 64] for h in range(ZH)]
                out_ref[k * XN + to, pl.ds(row, YN), :] = jnp.concatenate(both, axis=1)


def fold_kernel(in_ref, out_ref):
    total = in_ref[0]
    for i in range(1, CORES * XN):
        total = total + in_ref[i]
    turned = jnp.concatenate([total[:, 64:], total[:, :64]], axis=1)
    for b in range(4):
        for h, rows in enumerate((total, turned)):
            out_ref[h * YN : h * YN + YN, b, :] = rows[b * YN : b * YN + YN, :]


def ladder_part(left, right, amps):
    core = lax.axis_index("core")
    x = lax.axis_index("x")
    y = lax.axis_index("y")
    q, width = left.shape[0], right.shape[2]
    pairs = [(0, 1), (1, 0)]

    def quarter(s):
        to = lax.rem(x + s, XN)
        start = (0, (to // XD) * C_PART, lax.rem(to, XD) * D_PART)
        return jnp.transpose(lax.dynamic_slice(amps, start, (64, C_PART, D_PART)), (1, 0, 2))

    t_parts = [quarter(0)]
    for s in range(1, XN):
        t_parts.append(lax.ppermute(quarter(s), "x", [(i, (i + s) % XN) for i in range(XN)]))
    part = lax.dynamic_slice(right, (core * HALF, lax.rem(y, SLOTS), 0), (HALF, 1, width))
    part = jnp.transpose(part.reshape(HALF, XD, 2, LANES), (1, 2, 0, 3))
    part = jnp.broadcast_to(part[None, None], (ZN, XC, *part.shape)).reshape(ZN * XN, 2, HALF, LANES)
    r0 = exchange(part, ("zl", "x"))
    lt = jnp.transpose(left.reshape(q, ZHY, CORES, 16), (0, 3, 2, 1)).reshape(q, XC, 256)
    lt = jnp.broadcast_to(jnp.transpose(lt, (1, 0, 2))[None], (ZN, XC, q, 256))
    lt, r0 = lax.optimization_barrier((lt, r0))
    lz = exchange(lt, "zl")
    hops = (
        [(i, (i - 1) % YN) for i in range(YN)],
        [(i, (i + (2 if i % 2 == 0 else -2)) % YN) for i in range(YN)],
        [(i, (i + 1) % YN) for i in range(YN)],
    )
    mine = [r0] + [lax.ppermute(r0, "y", hop) for hop in hops]
    lx = jnp.broadcast_to(jnp.transpose(lz, (1, 0, 2, 3))[:, None], (XC, XD, ZN, q, 256)).reshape(XN, ZN, q, 256)
    first = lax.ppermute(r0, "core", pairs)
    lx, first, t_parts = lax.optimization_barrier((lx, first, t_parts))
    lx = exchange(lx, "x")
    other = [first] + [lax.ppermute(r, "core", pairs) for r in mine[1:]]
    vmem = pl.BlockSpec(memory_space=pltpu.VMEM)
    hbm = pl.BlockSpec(memory_space=pl.ANY)
    part = pl.pallas_call(
        ladder_kernel,
        out_shape=jax.ShapeDtypeStruct((CORES * XN, 32, LANES), jnp.float32),
        in_specs=[pl.BlockSpec(memory_space=pltpu.SMEM)] + [hbm] * 13,
        out_specs=vmem,
        scratch_shapes=[
            pltpu.VMEM(lx.shape, lx.dtype),
            pltpu.VMEM((2 * SLOTS, *r0.shape), r0.dtype),
            pltpu.VMEM((XN, C_PART, 64, D_PART), amps.dtype),
            pltpu.SemaphoreType.DMA((13,)),
        ],
        compiler_params=pltpu.CompilerParams(vmem_limit_bytes=KERNEL_VMEM),
        name="ladder",
    )(jnp.stack([core, y, x]), lx, *mine, *other, *t_parts)
    part = exchange(part, ("core", "x"))
    part = pl.pallas_call(
        fold_kernel,
        out_shape=jax.ShapeDtypeStruct((ZHY, 4, LANES), jnp.float32),
        in_specs=[vmem],
        out_specs=vmem,
        compiler_params=pltpu.CompilerParams(vmem_limit_bytes=4 * 1024 * 1024),
        name="fold",
    )(part)
    part = exchange(part, ("zh", "y")).sum(axis=0)[:, :64]
    return jnp.transpose(part, (1, 0))[:, None, :]


def solution(mesh):
    fine = Mesh(mesh.devices.reshape(ZH, YN, CORES, ZN, XN), ("zh", "y", "core", "zl", "x"))
    row, col = ("zh", "y", "core"), ("zl", "x")
    placed = (P(col, None, row), P(col, None, None), P(col, row, None))
    return jax.shard_map(ladder_part, mesh=fine, in_specs=placed, out_specs=P(col, row, None), check_vma=False)
```

time: 239 us -> 130 us (0.54)
  waiting for transfers between devices: 130 us -> 23.8 us
  starting transfers between devices: 15.6 us -> 55.9 us
  local copies, waits for them, and re-layouts: 32.4 us -> 8.05 us
  between operations: 13.5 us -> 0.3 us
  Pallas kernels: 0 us -> 5.53 us
  matrix products: 5.48 us -> 0 us
  blocking collectives: 39.5 us -> 34.6 us
    all_gather x1 -> x0, waiting for transfers between devices: 56.9 us -> none  [per_device(): right_full = lax.all_gather(right_factors, 'col', axis=0, tiled=True)]
    all_to_all x1 -> x3, waiting for transfers between devices: 72.9 us -> 17.3 us  [exchange(): return lax.all_to_all(x, axis, 0, 0, tiled=True)]
    ppermute x0 -> x10, starting transfers between devices: none -> 30.6 us  [the longest x3 11.2 us: ladder_part(): mine = [r0] + [lax.ppermute(r0, 'y', hop) for hop in hops]]
    unnamed x14 -> x30, local copies, waits for them, and re-layouts: 18 us -> 4.24 us
    all_to_all x1 -> x3, starting transfers between devices: 15.6 us -> 25.3 us  [exchange(): return lax.all_to_all(x, axis, 0, 0, tiled=True)]
    ppermute x0 -> x10, waiting for transfers between devices: none -> 6.5 us  [the longest x3 6.48 us: ladder_part(): mine = [r0] + [lax.ppermute(r0, 'y', hop) for hop in hops]]
    all_to_all x2 -> x0, local copies, waits for them, and re-layouts: 5.86 us -> none  [the longest x1 5.35 us: copy_for_each(): lax.all_to_all(jnp.broadcast_to(x[None], (peers, *x.shape)), axis, 0, 0,...]
    pallas_call x0 -> x2, Pallas kernels: none -> 5.53 us  [the longest x1 5.44 us: ladder_part(): pl.pallas_call(ladder_kernel, out_shape=jax.ShapeDtypeStruct((CORES * XN,...]
  transfers between devices with their start and end apart: 2 -> 13, of which waited for: 2 -> 3; matrix products, arithmetic and copies ran while one was open for 9% -> 2% of each run, Pallas kernels for 0% -> 0%
where the time goes in v1:
time: 130 us; the launch traced here: 129 us
  starting transfers between devices  55.9 us (43%)
  blocking collectives  34.6 us (27%)
  waiting for transfers between devices  23.8 us (18%)
  local copies, waits for them, and re-layouts  8.05 us (6%)
  Pallas kernels  5.53 us (4%)
    all_to_all x2, blocking collectives, exchange(): return lax.all_to_all(x, axis, 0, 0, tiled=True)  34.6 us
    all_to_all x3, starting transfers between devices, exchange(): return lax.all_to_all(x, axis, 0, 0, tiled=True)  25.3 us
    all_to_all x3, waiting for transfers between devices, exchange(): return lax.all_to_all(x, axis, 0, 0, tiled=True)  17.3 us
    ppermute x3, starting transfers between devices, ladder_part(): mine = [r0] + [lax.ppermute(r0, 'y', hop) for hop in hops]  11.2 us
    ppermute x3, starting transfers between devices, ladder_part(): lax.ppermute(quarter(s), 'x', [(i, (i + s) % XN) for i in range(XN)])  7.83 us
    ppermute x3, starting transfers between devices, ladder_part(): other = [first] + [lax.ppermute(r, 'core', pairs) for r in mine[1:]]  7.5 us
    ppermute x3, waiting for transfers between devices, ladder_part(): mine = [r0] + [lax.ppermute(r0, 'y', hop) for hop in hops]  6.48 us
    pallas_call x1, Pallas kernels, ladder_part(): pl.pallas_call(ladder_kernel, out_shape=jax.ShapeDtypeStruct((CORES * XN,...  5.44 us
  transfers between devices with their start and end apart: 13, of which 3 were waited for; matrix products, arithmetic and copies ran while one was open for 2% of the time, Pallas kernels for 0%

profile of v1, /device:TPU:1, one launch (start us, length us, event | category | flops | bytes accessed | tf_op | source)
XLA Modules:
  0.0 128.9 jit_solution(6233520022761912227)
XLA Ops:
  0.0 0.0 copy-start
  0.0 0.9 copy-done
  1.0 0.2 dynamic-slice_reduce_fusion
  1.2 0.8 broadcast_in_dim.9
  2.0 0.0 copy-start.12
  2.0 15.5 %all-to-all-start = ((bf16[24,2,32,128]{3,2,1,0:T(8,128)(2,1)}), bf16[24,2,32,128]{3,2,1,0:T(8,128)(2,1)S(1)}, u32[]{:S(2)}, u32[]{:S(2)}) async-start(bf16[24,2,32,128]{3,2,1,0:T(8,128)(2,1)} %bitcast.8), calls=%async_computation | async-start | bytes 786432 | tf_op jit(solution)/shard_map/all_to_all | solution.py:20
  17.5 0.0 copy-start.3
  17.5 0.0 copy-done.12
  17.5 0.1 copy.15
  17.6 0.1 copy.16
  17.7 17.3 %all-to-all-done.refs_1_ = bf16[24,2,32,128]{3,2,1,0:T(8,128)(2,1)S(1)} async-done(((bf16[24,2,32,128]{3,2,1,0:T(8,128)(2,1)}), bf16[24,2,32,128]{3,2,1,0:T(8,128)(2,1)S(1)}, u32[]{:S(2)}, u32[]{:S(2)}) %all-to-all-start) | async-done | bytes 393248 | tf_op jit(solution)/shard_map/all_to_all | solution.py:20
  35.0 0.0 copy-start.2
  35.0 0.8 broadcast_in_dim.8
  35.9 6.0 %all-to-all-start.1 = ((bf16[6,2,64,256]{3,2,1,0:T(8,128)(2,1)}), bf16[6,2,64,256]{3,2,1,0:T(8,128)(2,1)S(1)}, u32[]{:S(2)}, u32[]{:S(2)}) async-start(bf16[6,2,64,256]{3,2,1,0:T(8,128)(2,1)} %broadcast_in_dim.8), calls=%async_computation.1 | async-start | bytes 786432 | tf_op jit(solution)/shard_map/all_to_all | solution.py:20
  41.8 0.0 copy-done.3
  41.8 0.1 constant_dynamic-slice_fusion
  42.0 1.9 %collective-permute-start.1 = (bf16[8,64,256]{2,1,0:T(8,128)(2,1)S(1)}, bf16[8,64,256]{2,1,0:T(8,128)(2,1)S(1)}, u32[]{:S(2)}, u32[]{:S(2)}) collective-permute-start(bf16[8,64,256]{2,1,0:T(8,128)(2,1)S(1)} %bitcast.34), channel_id=1, source_target_pairs={{0,1},{1,2},{2,3},{3,0},{4,5},{5,6},{6,7},{7,4},{8,9},{9,10},{10,1... | collective-permute-start | bytes 786440 | tf_op jit(solution)/shard_map/ppermute | solution.py:95
  44.0 3.3 %collective-permute-start.2 = (bf16[8,64,256]{2,1,0:T(8,128)(2,1)S(1)}, bf16[8,64,256]{2,1,0:T(8,128)(2,1)}, u32[]{:S(2)}, u32[]{:S(2)}) collective-permute-start(bf16[8,64,256]{2,1,0:T(8,128)(2,1)S(1)} %bitcast.33), channel_id=1, source_target_pairs={{0,2},{1,3},{2,0},{3,1},{4,6},{5,7},{6,4},{7,5},{8,10},{9,11},{10,... | collective-permute-start | bytes 786440 | tf_op jit(solution)/shard_map/ppermute | solution.py:95
  47.3 4.1 %collective-permute-start = (bf16[24,2,32,128]{3,2,1,0:T(8,128)(2,1)S(1)}, bf16[24,2,32,128]{3,2,1,0:T(8,128)(2,1)S(1)}, u32[]{:S(2)}, u32[]{:S(2)}) collective-permute-start(bf16[24,2,32,128]{3,2,1,0:T(8,128)(2,1)S(1)} %all-to-all-done.refs_1_), channel_id=1, source_target_pairs={{0,24},{24,0},{1,25},{25,1},{2,26},{26,2},{3,27},{27,3},{4,28},{28... | collective-permute-start | bytes 1179656 | tf_op jit(solution)/shard_map/ppermute | solution.py:111
  51.5 2.6 %collective-permute-start.3 = (bf16[8,64,256]{2,1,0:T(8,128)(2,1)S(1)}, bf16[8,64,256]{2,1,0:T(8,128)(2,1)}, u32[]{:S(2)}, u32[]{:S(2)}) collective-permute-start(bf16[8,64,256]{2,1,0:T(8,128)(2,1)S(1)} %bitcast.32), channel_id=1, source_target_pairs={{0,3},{1,0},{2,1},{3,2},{4,7},{5,4},{6,5},{7,6},{8,11},{9,8},{10,9... | collective-permute-start | bytes 786440 | tf_op jit(solution)/shard_map/ppermute | solution.py:95
  54.1 5.1 %collective-permute-start.4 = (bf16[24,2,32,128]{3,2,1,0:T(8,128)(2,1)S(1)}, bf16[24,2,32,128]{3,2,1,0:T(8,128)(2,1)S(1)}, u32[]{:S(2)}, u32[]{:S(2)}) collective-permute-start(bf16[24,2,32,128]{3,2,1,0:T(8,128)(2,1)S(1)} %all-to-all-done.refs_1_), channel_id=1, source_target_pairs={{0,336},{48,0},{96,48},{144,96},{192,144},{240,192},{288,240},{336... | collective-permute-start | bytes 1179656 | tf_op jit(solution)/shard_map/ppermute | solution.py:109
  59.2 0.0 collective-permute-done.1.refs_10_
  59.2 0.0 copy-start.11
  59.2 1.9 %collective-permute-start.5 = (bf16[24,2,32,128]{3,2,1,0:T(8,128)(2,1)S(1)}, bf16[24,2,32,128]{3,2,1,0:T(8,128)(2,1)S(1)}, u32[]{:S(2)}, u32[]{:S(2)}) collective-permute-start(bf16[24,2,32,128]{3,2,1,0:T(8,128)(2,1)S(1)} %all-to-all-done.refs_1_), channel_id=1, source_target_pairs={{0,96},{48,336},{96,192},{144,48},{192,288},{240,144},{288,0},{336... | collective-permute-start | bytes 1179656 | tf_op jit(solution)/shard_map/ppermute | solution.py:109
  61.1 0.0 collective-permute-done.2.refs_11_
  61.1 0.0 copy-done.2
  61.1 4.1 %collective-permute-start.6 = (bf16[24,2,32,128]{3,2,1,0:T(8,128)(2,1)S(1)}, bf16[24,2,32,128]{3,2,1,0:T(8,128)(2,1)S(1)}, u32[]{:S(2)}, u32[]{:S(2)}) collective-permute-start(bf16[24,2,32,128]{3,2,1,0:T(8,128)(2,1)S(1)} %all-to-all-done.refs_1_), channel_id=1, source_target_pairs={{0,48},{48,96},{96,144},{144,192},{192,240},{240,288},{288,336},{3... | collective-permute-start | bytes 1179656 | tf_op jit(solution)/shard_map/ppermute | solution.py:109
  65.3 0.7 copy.34
  66.1 0.0 copy-done.11
  66.1 0.0 all-to-all-done.1
  66.1 0.0 collective-permute-done.3.refs_12_
  66.1 0.0 collective-permute-done.refs_5_
  66.1 0.0 copy-start.4
  66.1 1.0 broadcast_in_dim.10
  67.1 0.0 copy-done.4
  67.1 3.9 %all-to-all-start.2 = ((bf16[4,6,64,256]{3,2,1,0:T(8,128)(2,1)}), bf16[4,6,64,256]{3,2,1,0:T(8,128)(2,1)S(1)}, u32[]{:S(2)}, u32[]{:S(2)}) async-start(bf16[4,6,64,256]{3,2,1,0:T(8,128)(2,1)} %bitcast.10), calls=%async_computation.2 | async-start | bytes 1572864 | tf_op jit(solution)/shard_map/all_to_all | solution.py:20
  71.0 4.6 %collective-permute-done.4.refs_2_ = bf16[24,2,32,128]{3,2,1,0:T(8,128)(2,1)S(1)} collective-permute-done((bf16[24,2,32,128]{3,2,1,0:T(8,128)(2,1)S(1)}, bf16[24,2,32,128]{3,2,1,0:T(8,128)(2,1)S(1)}, u32[]{:S(2)}, u32[]{:S(2)}) %collective-permute-start.4) | collective-permute-done | bytes 393248 | tf_op jit(solution)/shard_map/ppermute | solution.py:109
  75.6 0.0 copy-start.5
  75.6 3.2 %collective-permute-start.7 = (bf16[24,2,32,128]{3,2,1,0:T(8,128)(2,1)S(1)}, bf16[24,2,32,128]{3,2,1,0:T(8,128)(2,1)S(1)}, u32[]{:S(2)}, u32[]{:S(2)}) collective-permute-start(bf16[24,2,32,128]{3,2,1,0:T(8,128)(2,1)S(1)} %collective-permute-done.4.refs_2_), channel_id=1, source_target_pairs={{0,24},{24,0},{1,25},{25,1},{2,26},{26,2},{3,27},{27,3},{4,28},{28... | collective-permute-start | bytes 1179656 | tf_op jit(solution)/shard_map/ppermute | solution.py:114
  78.8 0.0 collective-permute-done.5.refs_3_
  78.8 0.0 copy-start.6
  78.8 1.9 %collective-permute-start.8 = (bf16[24,2,32,128]{3,2,1,0:T(8,128)(2,1)S(1)}, bf16[24,2,32,128]{3,2,1,0:T(8,128)(2,1)S(1)}, u32[]{:S(2)}, u32[]{:S(2)}) collective-permute-start(bf16[24,2,32,128]{3,2,1,0:T(8,128)(2,1)S(1)} %collective-permute-done.5.refs_3_), channel_id=1, source_target_pairs={{0,24},{24,0},{1,25},{25,1},{2,26},{26,2},{3,27},{27,3},{4,28},{28... | collective-permute-start | bytes 1179656 | tf_op jit(solution)/shard_map/ppermute | solution.py:114
  80.8 1.9 %collective-permute-done.6.refs_4_ = bf16[24,2,32,128]{3,2,1,0:T(8,128)(2,1)S(1)} collective-permute-done((bf16[24,2,32,128]{3,2,1,0:T(8,128)(2,1)S(1)}, bf16[24,2,32,128]{3,2,1,0:T(8,128)(2,1)S(1)}, u32[]{:S(2)}, u32[]{:S(2)}) %collective-permute-start.6) | collective-permute-done | bytes 393248 | tf_op jit(solution)/shard_map/ppermute | solution.py:109
  82.7 0.0 copy-start.7
  82.7 2.4 %collective-permute-start.9 = (bf16[24,2,32,128]{3,2,1,0:T(8,128)(2,1)S(1)}, bf16[24,2,32,128]{3,2,1,0:T(8,128)(2,1)S(1)}, u32[]{:S(2)}, u32[]{:S(2)}) collective-permute-start(bf16[24,2,32,128]{3,2,1,0:T(8,128)(2,1)S(1)} %collective-permute-done.6.refs_4_), channel_id=1, source_target_pairs={{0,24},{24,0},{1,25},{25,1},{2,26},{26,2},{3,27},{27,3},{4,28},{28... | collective-permute-start | bytes 1179656 | tf_op jit(solution)/shard_map/ppermute | solution.py:114
  85.1 0.7 pad_add_fusion.where_ref
  85.7 0.0 collective-permute-done.7.refs_6_
  85.7 0.0 copy-start.8
  85.7 0.0 collective-permute-done.8.refs_7_
  85.7 0.0 copy-start.9
  85.7 0.8 copy-done.9
  86.5 0.0 collective-permute-done.9.refs_8_
  86.5 0.0 all-to-all-done.2.refs_0_
  86.5 0.0 copy-done.5
  86.5 0.0 copy-done.6
  86.5 0.0 copy-done.7
  86.6 0.0 copy-done.8
  86.6 0.7 copy-done.10
  87.3 0.9 copy-done.1
  88.1 5.4 %ladder.1 = f32[8,32,128]{2,1,0:T(8,128)} custom-call(s32[3]{0:T(128)} %pad_add_fusion.where_ref, bf16[4,6,64,256]{3,2,1,0:T(8,128)(2,1)} %copy-done.1, bf16[24,2,32,128]{3,2,1,0:T(8,128)(2,1)} %copy-done.2, bf16[24,2,32,128]{3,2,1,0:T(8,128)(2,1)} %copy-done.5, bf16[24,2,32,128]{3,2,1,0:T(8,128)(2,1)} %copy-done.6, bf16[24,2,32,128]{3,2,1,0:T(8,128)(2,1)} %copy-done.7, ...), custom_call_target="tpu_custom_call" | custom-call | tf_op jit(solution)/shard_map/ladder/pallas_call | solution.py:117
  93.6 9.6 %all_to_all.25.in_ref = f32[8,32,128]{2,1,0:T(8,128)S(1)} all-to-all(f32[8,32,128]{2,1,0:T(8,128)} %ladder.1), channel_id=1, replica_groups=mesh['zh'=2,'y'=8,'core'=2,'zl'=6,'x'=4] {'core','x'}, dimensions={0} | all-to-all | bytes 262144 | tf_op jit(solution)/shard_map/all_to_all | solution.py:20
  103.2 0.1 fold.1
  103.3 24.9 %all_to_all.26 = f32[16,4,128]{2,1,0:T(4,128)S(1)} all-to-all(f32[16,4,128]{2,1,0:T(4,128)S(1)} %fold.1), channel_id=1, replica_groups=mesh['zh'=2,'y'=8,'core'=2,'zl'=6,'x'=4] {'zh','y'}, dimensions={0} | all-to-all | bytes 65536 | tf_op jit(solution)/shard_map/all_to_all | solution.py:20
  128.3 0.6 slice_bitcast_fusion
  (9 shorter events, 0.2 us)
Async XLA Ops:
  0.0 1.0 copy-start
  2.0 15.5 %copy-start.12 = (bf16[64,32,16]{0,2,1:T(8,128)(2,1)S(1)}, bf16[64,32,16]{0,2,1:T(8,128)(2,1)}, u32[]{:S(2)}) copy-start(bf16[64,32,16]{0,2,1:T(8,128)(2,1)} %param.3) | copy-start | bytes 196612
  2.0 33.0 %all-to-all-start = ((bf16[24,2,32,128]{3,2,1,0:T(8,128)(2,1)}), bf16[24,2,32,128]{3,2,1,0:T(8,128)(2,1)S(1)}, u32[]{:S(2)}, u32[]{:S(2)}) async-start(bf16[24,2,32,128]{3,2,1,0:T(8,128)(2,1)} %bitcast.8), calls=%async_computation | async-start | bytes 786432 | tf_op jit(solution)/shard_map/all_to_all | solution.py:20
  17.5 24.3 %copy-start.3 = (bf16[64,16,512]{2,1,0:T(8,128)(2,1)S(1)}, bf16[64,16,512]{2,1,0:T(8,128)(2,1)}, u32[]{:S(2)}) copy-start(bf16[64,16,512]{2,1,0:T(8,128)(2,1)} %param.5) | copy-start | bytes 3145732
  35.0 26.1 %copy-start.2 = (bf16[24,2,32,128]{3,2,1,0:T(8,128)(2,1)}, bf16[24,2,32,128]{3,2,1,0:T(8,128)(2,1)S(1)}, u32[]{:S(2)}) copy-start(bf16[24,2,32,128]{3,2,1,0:T(8,128)(2,1)S(1)} %all-to-all-done.refs_1_) | copy-start | bytes 1179652
  35.9 30.2 %all-to-all-start.1 = ((bf16[6,2,64,256]{3,2,1,0:T(8,128)(2,1)}), bf16[6,2,64,256]{3,2,1,0:T(8,128)(2,1)S(1)}, u32[]{:S(2)}, u32[]{:S(2)}) async-start(bf16[6,2,64,256]{3,2,1,0:T(8,128)(2,1)} %broadcast_in_dim.8), calls=%async_computation.1 | async-start | bytes 786432 | tf_op jit(solution)/shard_map/all_to_all | solution.py:20
  42.0 17.2 %collective-permute-start.1 = (bf16[8,64,256]{2,1,0:T(8,128)(2,1)S(1)}, bf16[8,64,256]{2,1,0:T(8,128)(2,1)S(1)}, u32[]{:S(2)}, u32[]{:S(2)}) collective-permute-start(bf16[8,64,256]{2,1,0:T(8,128)(2,1)S(1)} %bitcast.34), channel_id=1, source_target_pairs={{0,1},{1,2},{2,3},{3,0},{4,5},{5,6},{6,7},{7,4},{8,9},{9,10},{10,1... | collective-permute-start | bytes 786440 | tf_op jit(solution)/shard_map/ppermute | solution.py:95
  44.0 17.1 %collective-permute-start.2 = (bf16[8,64,256]{2,1,0:T(8,128)(2,1)S(1)}, bf16[8,64,256]{2,1,0:T(8,128)(2,1)}, u32[]{:S(2)}, u32[]{:S(2)}) collective-permute-start(bf16[8,64,256]{2,1,0:T(8,128)(2,1)S(1)} %bitcast.33), channel_id=1, source_target_pairs={{0,2},{1,3},{2,0},{3,1},{4,6},{5,7},{6,4},{7,5},{8,10},{9,11},{10,... | collective-permute-start | bytes 786440 | tf_op jit(solution)/shard_map/ppermute | solution.py:95
  47.3 18.8 %collective-permute-start = (bf16[24,2,32,128]{3,2,1,0:T(8,128)(2,1)S(1)}, bf16[24,2,32,128]{3,2,1,0:T(8,128)(2,1)S(1)}, u32[]{:S(2)}, u32[]{:S(2)}) collective-permute-start(bf16[24,2,32,128]{3,2,1,0:T(8,128)(2,1)S(1)} %all-to-all-done.refs_1_), channel_id=1, source_target_pairs={{0,24},{24,0},{1,25},{25,1},{2,26},{26,2},{3,27},{27,3},{4,28},{28... | collective-permute-start | bytes 1179656 | tf_op jit(solution)/shard_map/ppermute | solution.py:111
  51.5 14.6 %collective-permute-start.3 = (bf16[8,64,256]{2,1,0:T(8,128)(2,1)S(1)}, bf16[8,64,256]{2,1,0:T(8,128)(2,1)}, u32[]{:S(2)}, u32[]{:S(2)}) collective-permute-start(bf16[8,64,256]{2,1,0:T(8,128)(2,1)S(1)} %bitcast.32), channel_id=1, source_target_pairs={{0,3},{1,0},{2,1},{3,2},{4,7},{5,4},{6,5},{7,6},{8,11},{9,8},{10,9... | collective-permute-start | bytes 786440 | tf_op jit(solution)/shard_map/ppermute | solution.py:95
  54.1 21.5 %collective-permute-start.4 = (bf16[24,2,32,128]{3,2,1,0:T(8,128)(2,1)S(1)}, bf16[24,2,32,128]{3,2,1,0:T(8,128)(2,1)S(1)}, u32[]{:S(2)}, u32[]{:S(2)}) collective-permute-start(bf16[24,2,32,128]{3,2,1,0:T(8,128)(2,1)S(1)} %all-to-all-done.refs_1_), channel_id=1, source_target_pairs={{0,336},{48,0},{96,48},{144,96},{192,144},{240,192},{288,240},{336... | collective-permute-start | bytes 1179656 | tf_op jit(solution)/shard_map/ppermute | solution.py:109
  59.2 6.9 %copy-start.11 = (bf16[8,64,256]{2,1,0:T(8,128)(2,1)}, bf16[8,64,256]{2,1,0:T(8,128)(2,1)S(1)}, u32[]{:S(2)}) copy-start(bf16[8,64,256]{2,1,0:T(8,128)(2,1)S(1)} %collective-permute-done.1.refs_10_) | copy-start | bytes 786436
  59.2 19.6 %collective-permute-start.5 = (bf16[24,2,32,128]{3,2,1,0:T(8,128)(2,1)S(1)}, bf16[24,2,32,128]{3,2,1,0:T(8,128)(2,1)S(1)}, u32[]{:S(2)}, u32[]{:S(2)}) collective-permute-start(bf16[24,2,32,128]{3,2,1,0:T(8,128)(2,1)S(1)} %all-to-all-done.refs_1_), channel_id=1, source_target_pairs={{0,96},{48,336},{96,192},{144,48},{192,288},{240,144},{288,0},{336... | collective-permute-start | bytes 1179656 | tf_op jit(solution)/shard_map/ppermute | solution.py:109
  61.1 21.5 %collective-permute-start.6 = (bf16[24,2,32,128]{3,2,1,0:T(8,128)(2,1)S(1)}, bf16[24,2,32,128]{3,2,1,0:T(8,128)(2,1)S(1)}, u32[]{:S(2)}, u32[]{:S(2)}) collective-permute-start(bf16[24,2,32,128]{3,2,1,0:T(8,128)(2,1)S(1)} %all-to-all-done.refs_1_), channel_id=1, source_target_pairs={{0,48},{48,96},{96,144},{144,192},{192,240},{240,288},{288,336},{3... | collective-permute-start | bytes 1179656 | tf_op jit(solution)/shard_map/ppermute | solution.py:109
  66.1 1.0 copy-start.4
  67.1 19.4 %all-to-all-start.2 = ((bf16[4,6,64,256]{3,2,1,0:T(8,128)(2,1)}), bf16[4,6,64,256]{3,2,1,0:T(8,128)(2,1)S(1)}, u32[]{:S(2)}, u32[]{:S(2)}) async-start(bf16[4,6,64,256]{3,2,1,0:T(8,128)(2,1)} %bitcast.10), calls=%async_computation.2 | async-start | bytes 1572864 | tf_op jit(solution)/shard_map/all_to_all | solution.py:20
  75.6 10.9 %copy-start.5 = (bf16[24,2,32,128]{3,2,1,0:T(8,128)(2,1)}, bf16[24,2,32,128]{3,2,1,0:T(8,128)(2,1)S(1)}, u32[]{:S(2)}) copy-start(bf16[24,2,32,128]{3,2,1,0:T(8,128)(2,1)S(1)} %collective-permute-done.4.refs_2_) | copy-start | bytes 1179652
  75.6 10.1 %collective-permute-start.7 = (bf16[24,2,32,128]{3,2,1,0:T(8,128)(2,1)S(1)}, bf16[24,2,32,128]{3,2,1,0:T(8,128)(2,1)S(1)}, u32[]{:S(2)}, u32[]{:S(2)}) collective-permute-start(bf16[24,2,32,128]{3,2,1,0:T(8,128)(2,1)S(1)} %collective-permute-done.4.refs_2_), channel_id=1, source_target_pairs={{0,24},{24,0},{1,25},{25,1},{2,26},{26,2},{3,27},{27,3},{4,28},{28... | collective-permute-start | bytes 1179656 | tf_op jit(solution)/shard_map/ppermute | solution.py:114
  78.8 7.7 %copy-start.6 = (bf16[24,2,32,128]{3,2,1,0:T(8,128)(2,1)}, bf16[24,2,32,128]{3,2,1,0:T(8,128)(2,1)S(1)}, u32[]{:S(2)}) copy-start(bf16[24,2,32,128]{3,2,1,0:T(8,128)(2,1)S(1)} %collective-permute-done.5.refs_3_) | copy-start | bytes 1179652
  78.8 6.9 %collective-permute-start.8 = (bf16[24,2,32,128]{3,2,1,0:T(8,128)(2,1)S(1)}, bf16[24,2,32,128]{3,2,1,0:T(8,128)(2,1)S(1)}, u32[]{:S(2)}, u32[]{:S(2)}) collective-permute-start(bf16[24,2,32,128]{3,2,1,0:T(8,128)(2,1)S(1)} %collective-permute-done.5.refs_3_), channel_id=1, source_target_pairs={{0,24},{24,0},{1,25},{25,1},{2,26},{26,2},{3,27},{27,3},{4,28},{28... | collective-permute-start | bytes 1179656 | tf_op jit(solution)/shard_map/ppermute | solution.py:114
  82.7 3.9 %copy-start.7 = (bf16[24,2,32,128]{3,2,1,0:T(8,128)(2,1)}, bf16[24,2,32,128]{3,2,1,0:T(8,128)(2,1)S(1)}, u32[]{:S(2)}) copy-start(bf16[24,2,32,128]{3,2,1,0:T(8,128)(2,1)S(1)} %collective-permute-done.6.refs_4_) | copy-start | bytes 1179652
  82.7 3.9 %collective-permute-start.9 = (bf16[24,2,32,128]{3,2,1,0:T(8,128)(2,1)S(1)}, bf16[24,2,32,128]{3,2,1,0:T(8,128)(2,1)S(1)}, u32[]{:S(2)}, u32[]{:S(2)}) collective-permute-start(bf16[24,2,32,128]{3,2,1,0:T(8,128)(2,1)S(1)} %collective-permute-done.6.refs_4_), channel_id=1, source_target_pairs={{0,24},{24,0},{1,25},{25,1},{2,26},{26,2},{3,27},{27,3},{4,28},{28... | collective-permute-start | bytes 1179656 | tf_op jit(solution)/shard_map/ppermute | solution.py:114
  85.7 0.9 copy-start.8
  85.7 0.8 copy-start.9
  86.5 0.7 copy-start.10
  87.3 0.9 copy-start.1

commit v2 on v1

v2 whole, which is shorter than its diff:
```python
import jax
import jax.numpy as jnp
from jax import lax
from jax.experimental import pallas as pl
from jax.experimental.pallas import tpu as pltpu
from jax.sharding import Mesh, PartitionSpec as P


LANES = 128
ZH, YN, CORES, ZN, XN = 2, 8, 2, 6, 4
ZHY = ZH * YN
HALF = 32
SLOTS = 4
L_ROWS = 256
KERNEL_VMEM = 50 * 1024 * 1024


def exchange(x, axis):
    return lax.all_to_all(x, axis, 0, 0, tiled=True)


def ladder_kernel(where_ref, left_ref, r0_ref, r1_ref, o0_ref, o1_ref, *refs):
    amps_hbm, out_ref, (amps_ref, sems) = refs[:XN], refs[XN], refs[XN + 1 :]
    core, y, x = where_ref[0], where_ref[1], where_ref[2]
    copies = [pltpu.make_async_copy(t, amps_ref.at[s], sems.at[s]) for s, t in enumerate(amps_hbm)]
    for copy in copies:
        copy.start()

    def left_of(half):
        cols = []
        for j in range(4):
            start = pl.multiple_of(j * 64 + half * HALF, HALF)
            rows = [left_ref[i, z, pl.ds(start, HALF), :] for z in range(ZN) for i in range(XN)]
            cols.append(jnp.concatenate(rows, axis=0))
        return jnp.concatenate(cols, axis=1)

    def right_of(own, rest):
        return jnp.concatenate([own[...]] + [rest[i] for i in range(SLOTS - 1)], axis=1)

    dims = (((0,), (0,)), ((), ()))
    ints = lax.dot_general(left_of(core), right_of(r0_ref, r1_ref), dims, preferred_element_type=jnp.float32)
    ints = ints + lax.dot_general(left_of(1 - core), right_of(o0_ref, o1_ref), dims, preferred_element_type=jnp.float32)
    ints = ints.astype(jnp.bfloat16)
    for copy in copies:
        copy.wait()
    acc = jnp.zeros((LANES, 256), jnp.float32)
    for c in range(0, 16, 2):
        pair = []
        for k in (c, c + 1):
            cols = [ints[k * 32 : k * 32 + 32, i * LANES : (i + 1) * LANES] for i in range(SLOTS)]
            pair.append(jnp.concatenate(cols, axis=0))
        amps = [jnp.concatenate([amps_ref[s, k] for s in range(XN)], axis=0) for k in (c, c + 1)]
        acc = acc + lax.dot_general(
            jnp.concatenate(pair, axis=1),
            jnp.concatenate(amps, axis=1),
            (((1,), (1,)), ((), ())),
            preferred_element_type=jnp.float32,
        )
    for slot in range(SLOTS):
        row = pl.multiple_of(lax.rem(y + slot, SLOTS) * YN, YN)
        for s in range(XN):
            to = lax.rem(x + XN - s, XN)
            for k in range(CORES):
                r = slot * 32 + k * 16
                both = [acc[r + h * YN : r + h * YN + YN, s * 64 : s * 64 + 64] for h in range(ZH)]
                out_ref[k * XN + to, pl.ds(row, YN), :] = jnp.concatenate(both, axis=1)


def fold_kernel(in_ref, out_ref):
    total = in_ref[0]
    for i in range(1, CORES * XN):
        total = total + in_ref[i]
    turned = jnp.concatenate([total[:, 64:], total[:, :64]], axis=1)
    for b in range(4):
        for h, rows in enumerate((total, turned)):
            out_ref[h * YN : h * YN + YN, b, :] = rows[b * YN : b * YN + YN, :]


def ladder_part(left, right, amps):
    core = lax.axis_index("core")
    x = lax.axis_index("x")
    y = lax.axis_index("y")
    q, width = left.shape[0], right.shape[2]
    pairs = [(0, 1), (1, 0)]

    part = lax.dynamic_slice(right, (core * HALF, lax.rem(y, SLOTS), 0), (HALF, 1, width))
    part = jnp.transpose(part.reshape(HALF, XN, LANES), (1, 0, 2))
    rx = exchange(part, "x").reshape(1, XN * HALF, LANES)

    def quarter(s):
        start = lax.rem(x + s, XN) * LANES
        return jnp.transpose(lax.dynamic_slice_in_dim(amps, start, LANES, axis=2), (1, 0, 2))

    t_parts = [quarter(0)]
    for s in range(1, XN):
        t_parts.append(lax.ppermute(quarter(s), "x", [(i, (i + s) % XN) for i in range(XN)]))
    lt = jnp.transpose(left.reshape(q, ZHY, CORES, 16), (0, 3, 2, 1)).reshape(q, 4, LANES)
    lt = jnp.transpose(lt, (1, 0, 2)).reshape(1, L_ROWS, LANES)
    both = jnp.concatenate([lt, rx], axis=1)
    both = exchange(jnp.broadcast_to(both, (ZN, *both.shape[1:])), "zl")
    r0 = both[:, L_ROWS:].reshape(ZN * XN * HALF, LANES)
    lx = jnp.broadcast_to(both[None, :, :L_ROWS], (XN, ZN, L_ROWS, LANES))
    lx, r0, t_parts = lax.optimization_barrier((lx, r0, t_parts))
    lx = exchange(lx, "x")
    hops = (
        [(i, (i - 1) % YN) for i in range(YN)],
        [(i, (i + (2 if i % 2 == 0 else -2)) % YN) for i in range(YN)],
        [(i, (i + 1) % YN) for i in range(YN)],
    )
    r1 = [lax.ppermute(r0, "y", hop) for hop in hops]
    o0 = lax.ppermute(r0, "core", pairs)
    r1 = jnp.stack(r1)
    o1 = lax.ppermute(r1, "core", pairs)
    vmem = pl.BlockSpec(memory_space=pltpu.VMEM)
    hbm = pl.BlockSpec(memory_space=pl.ANY)
    part = pl.pallas_call(
        ladder_kernel,
        out_shape=jax.ShapeDtypeStruct((CORES * XN, 32, LANES), jnp.float32),
        in_specs=[pl.BlockSpec(memory_space=pltpu.SMEM)] + [vmem] * 5 + [hbm] * XN,
        out_specs=vmem,
        scratch_shapes=[
            pltpu.VMEM((XN, 16, 64, LANES), amps.dtype),
            pltpu.SemaphoreType.DMA((XN,)),
        ],
        compiler_params=pltpu.CompilerParams(vmem_limit_bytes=KERNEL_VMEM),
        name="ladder",
    )(jnp.stack([core, y, x]), lx, r0, r1, o0, o1, *t_parts)
    part = exchange(part, ("core", "x"))
    part = pl.pallas_call(
        fold_kernel,
        out_shape=jax.ShapeDtypeStruct((ZHY, 4, LANES), jnp.float32),
        in_specs=[vmem],
        out_specs=vmem,
        compiler_params=pltpu.CompilerParams(vmem_limit_bytes=4 * 1024 * 1024),
        name="fold",
    )(part)
    part = exchange(part, ("zh", "y")).sum(axis=0)[:, :64]
    return jnp.transpose(part, (1, 0))[:, None, :]


def solution(mesh):
    fine = Mesh(mesh.devices.reshape(ZH, YN, CORES, ZN, XN), ("zh", "y", "core", "zl", "x"))
    row, col = ("zh", "y", "core"), ("zl", "x")
    placed = (P(col, None, row), P(col, None, None), P(col, row, None))
    return jax.shard_map(ladder_part, mesh=fine, in_specs=placed, out_specs=P(col, row, None), check_vma=False)
```

time: 130 us -> 118 us (0.908)
  starting transfers between devices: 55.9 us -> 46.8 us
  blocking collectives: 34.6 us -> 37.1 us
  Pallas kernels: 5.53 us -> 3.67 us
  local copies, waits for them, and re-layouts: 8.05 us -> 6.37 us
    ppermute x7 -> x5, starting transfers between devices: 22.8 us -> 16.9 us  [the longest x3 11.2 us: ladder_part(): r1 = [lax.ppermute(r0, 'y', hop) for hop in hops]]
    all_to_all x3, starting transfers between devices: 25.3 us -> 21 us  [exchange(): return lax.all_to_all(x, axis, 0, 0, tiled=True)]
    unnamed x30 -> x8, local copies, waits for them, and re-layouts: 4.24 us -> 1.23 us
    all_to_all x2, blocking collectives: 34.6 us -> 37.1 us  [exchange(): return lax.all_to_all(x, axis, 0, 0, tiled=True)]
    pallas_call x1, Pallas kernels: 5.44 us -> 3.58 us  [ladder_part(): pl.pallas_call(ladder_kernel, out_shape=jax.ShapeDtypeStruct((CORES * XN,...]
    broadcast_in_dim x3 -> x2, local copies, waits for them, and re-layouts: 2.69 us -> 2.38 us  [the longest x1 1.5 us: ladder_part(): lx = jnp.broadcast_to(both[None, :, :L_ROWS], (XN, ZN, L_ROWS, LANES))]
    ppermute x7 -> x5, waiting for transfers between devices: 6.49 us -> 6.49 us  [the longest x3 5.16 us: ladder_part(): r1 = [lax.ppermute(r0, 'y', hop) for hop in hops]]
  transfers between devices with their start and end apart: 13 -> 11, of which waited for: 3 -> 5; matrix products, arithmetic and copies ran while one was open for 2% -> 2% of each run, Pallas kernels for 0% -> 0%
where the time goes in v2:
time: 118 us; the launch traced here: 117 us
  starting transfers between devices  46.8 us (40%)
  blocking collectives  37.1 us (31%)
  waiting for transfers between devices  22.9 us (19%)
  local copies, waits for them, and re-layouts  6.37 us (5%)
  Pallas kernels  3.67 us (3%)
    all_to_all x2, blocking collectives, exchange(): return lax.all_to_all(x, axis, 0, 0, tiled=True)  37.1 us
    all_to_all x3, starting transfers between devices, exchange(): return lax.all_to_all(x, axis, 0, 0, tiled=True)  21 us
    all_to_all x3, waiting for transfers between devices, exchange(): return lax.all_to_all(x, axis, 0, 0, tiled=True)  16.4 us
    ppermute x3, starting transfers between devices, ladder_part(): r1 = [lax.ppermute(r0, 'y', hop) for hop in hops]  11.2 us
    ppermute x3, starting transfers between devices, ladder_part(): lax.ppermute(quarter(s), 'x', [(i, (i + s) % XN) for i in range(XN)])  8.89 us
    ppermute x3, waiting for transfers between devices, ladder_part(): r1 = [lax.ppermute(r0, 'y', hop) for hop in hops]  5.16 us
    ppermute x1, starting transfers between devices, ladder_part(): o1 = lax.ppermute(r1, 'core', pairs)  3.81 us
    pallas_call x1, Pallas kernels, ladder_part(): pl.pallas_call(ladder_kernel, out_shape=jax.ShapeDtypeStruct((CORES * XN,...  3.58 us
  transfers between devices with their start and end apart: 11, of which 5 were waited for; matrix products, arithmetic and copies ran while one was open for 2% of the time, Pallas kernels for 0%

profile of v2, /device:TPU:1, one launch (start us, length us, event | category | flops | bytes accessed | tf_op | source)
XLA Modules:
  0.0 117.2 jit_solution(17402995437300695505)
XLA Ops:
  0.0 0.0 copy-start
  0.0 0.0 copy-start.1
  0.0 0.9 copy-done
  1.0 0.2 dynamic-slice_reduce_fusion
  1.2 0.6 copy.22
  1.8 4.8 %all-to-all-start = ((bf16[4,32,128]{2,1,0:T(8,128)(2,1)}), bf16[4,32,128]{2,1,0:T(8,128)(2,1)S(1)}, u32[]{:S(2)}, u32[]{:S(2)}) async-start(bf16[4,32,128]{2,1,0:T(8,128)(2,1)} %copy.22), calls=%async_computation | async-start | bytes 65536 | tf_op jit(solution)/shard_map/all_to_all | solution.py:19
  6.6 1.0 copy.20
  7.6 0.1 copy.21
  7.7 3.2 %all-to-all-done = bf16[4,32,128]{2,1,0:T(8,128)(2,1)S(1)} async-done(((bf16[4,32,128]{2,1,0:T(8,128)(2,1)}), bf16[4,32,128]{2,1,0:T(8,128)(2,1)S(1)}, u32[]{:S(2)}, u32[]{:S(2)}) %all-to-all-start) | async-done | bytes 32800 | tf_op jit(solution)/shard_map/all_to_all | solution.py:19
  10.9 0.9 broadcast_in_dim.17
  11.8 11.8 %all-to-all-start.1 = ((bf16[6,384,128]{2,1,0:T(8,128)(2,1)}), bf16[6,384,128]{2,1,0:T(8,128)(2,1)S(1)}, u32[]{:S(2)}, u32[]{:S(2)}) async-start(bf16[6,384,128]{2,1,0:T(8,128)(2,1)} %broadcast_in_dim.17), calls=%async_computation.1 | async-start | bytes 1179648 | tf_op jit(solution)/shard_map/all_to_all | solution.py:19
  23.6 0.0 copy-done.1
  23.6 0.3 constant_dynamic-slice_fusion
  23.9 0.1 copy.37
  24.0 2.2 %collective-permute-start = (bf16[16,64,128]{2,1,0:T(8,128)(2,1)S(1)}, bf16[16,64,128]{2,1,0:T(8,128)(2,1)S(1)}, u32[]{:S(2)}, u32[]{:S(2)}) collective-permute-start(bf16[16,64,128]{2,1,0:T(8,128)(2,1)S(1)} %bitcast.42), channel_id=1, source_target_pairs={{0,1},{1,2},{2,3},{3,0},{4,5},{5,6},{6,7},{7,4},{8,9},{9,10},{10,1... | collective-permute-start | bytes 786440 | tf_op jit(solution)/shard_map/ppermute | solution.py:96
  26.2 0.1 copy.36
  26.2 3.7 %collective-permute-start.1 = (bf16[16,64,128]{2,1,0:T(8,128)(2,1)S(1)}, bf16[16,64,128]{2,1,0:T(8,128)(2,1)S(1)}, u32[]{:S(2)}, u32[]{:S(2)}) collective-permute-start(bf16[16,64,128]{2,1,0:T(8,128)(2,1)S(1)} %bitcast.43), channel_id=1, source_target_pairs={{0,2},{1,3},{2,0},{3,1},{4,6},{5,7},{6,4},{7,5},{8,10},{9,11},{10,... | collective-permute-start | bytes 786440 | tf_op jit(solution)/shard_map/ppermute | solution.py:96
  29.9 0.1 copy.35
  30.0 3.0 %collective-permute-start.2 = (bf16[16,64,128]{2,1,0:T(8,128)(2,1)S(1)}, bf16[16,64,128]{2,1,0:T(8,128)(2,1)S(1)}, u32[]{:S(2)}, u32[]{:S(2)}) collective-permute-start(bf16[16,64,128]{2,1,0:T(8,128)(2,1)S(1)} %bitcast.44), channel_id=1, source_target_pairs={{0,3},{1,0},{2,1},{3,2},{4,7},{5,4},{6,5},{7,6},{8,11},{9,8},{10,9... | collective-permute-start | bytes 786440 | tf_op jit(solution)/shard_map/ppermute | solution.py:96
  33.0 0.1 copy.38
  33.1 13.2 %all-to-all-done.1 = bf16[6,384,128]{2,1,0:T(8,128)(2,1)S(1)} async-done(((bf16[6,384,128]{2,1,0:T(8,128)(2,1)}), bf16[6,384,128]{2,1,0:T(8,128)(2,1)S(1)}, u32[]{:S(2)}, u32[]{:S(2)}) %all-to-all-start.1) | async-done | bytes 589856 | tf_op jit(solution)/shard_map/all_to_all | solution.py:19
  46.3 0.0 collective-permute-done.refs_1_
  46.4 0.0 collective-permute-done.1.refs_2_
  46.4 0.0 collective-permute-done.2.refs_3_
  46.4 1.5 %broadcast_in_dim.18 = bf16[4,6,256,128]{3,2,1,0:T(8,128)(2,1)} broadcast(bf16[6,256,128]{2,1,0:T(8,128)(2,1)S(1)} %slice.12), dimensions={1,2,3} | broadcast | bytes 1966080 | tf_op jit(solution)/shard_map/broadcast_in_dim | solution.py:102
  47.9 4.3 %all-to-all-start.2 = ((bf16[4,6,256,128]{3,2,1,0:T(8,128)(2,1)}), bf16[4,6,256,128]{3,2,1,0:T(8,128)(2,1)}, u32[]{:S(2)}, u32[]{:S(2)}) async-start(bf16[4,6,256,128]{3,2,1,0:T(8,128)(2,1)} %broadcast_in_dim.18), calls=%async_computation.2 | async-start | bytes 3145728 | tf_op jit(solution)/shard_map/all_to_all | solution.py:19
  52.2 3.2 %collective-permute-start.5 = (bf16[768,128]{1,0:T(8,128)(2,1)S(1)}, bf16[768,128]{1,0:T(8,128)(2,1)S(1)}, u32[]{:S(2)}, u32[]{:S(2)}) collective-permute-start(bf16[768,128]{1,0:T(8,128)(2,1)S(1)} %bitcast.35), channel_id=1, source_target_pairs={{0,48},{48,96},{96,144},{144,192},{192,240},{240,288},{288,336},{3... | collective-permute-start | bytes 589832 | tf_op jit(solution)/shard_map/ppermute | solution.py:110
  55.4 4.2 %collective-permute-start.4 = (bf16[768,128]{1,0:T(8,128)(2,1)S(1)}, bf16[768,128]{1,0:T(8,128)(2,1)S(1)}, u32[]{:S(2)}, u32[]{:S(2)}) collective-permute-start(bf16[768,128]{1,0:T(8,128)(2,1)S(1)} %bitcast.36), channel_id=1, source_target_pairs={{0,96},{48,336},{96,192},{144,48},{192,288},{240,144},{288,0},{336... | collective-permute-start | bytes 589832 | tf_op jit(solution)/shard_map/ppermute | solution.py:110
  59.7 3.7 %collective-permute-start.3 = (bf16[768,128]{1,0:T(8,128)(2,1)S(1)}, bf16[768,128]{1,0:T(8,128)(2,1)S(1)}, u32[]{:S(2)}, u32[]{:S(2)}) collective-permute-start(bf16[768,128]{1,0:T(8,128)(2,1)S(1)} %bitcast.37), channel_id=1, source_target_pairs={{0,336},{48,0},{96,48},{144,96},{192,144},{240,192},{288,240},{336... | collective-permute-start | bytes 589832 | tf_op jit(solution)/shard_map/ppermute | solution.py:110
  63.4 0.0 collective-permute-done.5
  63.4 2.9 %collective-permute-done.4 = bf16[768,128]{1,0:T(8,128)(2,1)S(1)} collective-permute-done((bf16[768,128]{1,0:T(8,128)(2,1)S(1)}, bf16[768,128]{1,0:T(8,128)(2,1)S(1)}, u32[]{:S(2)}, u32[]{:S(2)}) %collective-permute-start.4) | collective-permute-done | bytes 196640 | tf_op jit(solution)/shard_map/ppermute | solution.py:110
  66.4 2.2 %collective-permute-done.3 = bf16[768,128]{1,0:T(8,128)(2,1)S(1)} collective-permute-done((bf16[768,128]{1,0:T(8,128)(2,1)S(1)}, bf16[768,128]{1,0:T(8,128)(2,1)S(1)}, u32[]{:S(2)}, u32[]{:S(2)}) %collective-permute-start.3) | collective-permute-done | bytes 196640 | tf_op jit(solution)/shard_map/ppermute | solution.py:110
  68.6 0.1 pad_maximum_fusion.r1_ref
  68.6 3.8 %collective-permute-start.7 = (bf16[3,768,128]{2,1,0:T(8,128)(2,1)S(1)}, bf16[3,768,128]{2,1,0:T(8,128)(2,1)S(1)}, u32[]{:S(2)}, u32[]{:S(2)}) collective-permute-start(bf16[3,768,128]{2,1,0:T(8,128)(2,1)S(1)} %pad_maximum_fusion.r1_ref), channel_id=1, source_target_pairs={{0,24},{24,0},{1,25},{25,1},{2,26},{26,2},{3,27},{27,3},{4,28},{28... | collective-permute-start | bytes 1769480 | tf_op jit(solution)/shard_map/ppermute | solution.py:113
  72.5 1.9 %collective-permute-start.6 = (bf16[768,128]{1,0:T(8,128)(2,1)S(1)}, bf16[768,128]{1,0:T(8,128)(2,1)S(1)}, u32[]{:S(2)}, u32[]{:S(2)}) collective-permute-start(bf16[768,128]{1,0:T(8,128)(2,1)S(1)} %bitcast.38), channel_id=1, source_target_pairs={{0,24},{24,0},{1,25},{25,1},{2,26},{26,2},{3,27},{27,3},{4,28},{28... | collective-permute-start | bytes 589832 | tf_op jit(solution)/shard_map/ppermute | solution.py:111
  74.4 0.1 pad_add_fusion.where_ref
  74.5 1.3 %collective-permute-done.6.o0_ref = bf16[768,128]{1,0:T(8,128)(2,1)S(1)} collective-permute-done((bf16[768,128]{1,0:T(8,128)(2,1)S(1)}, bf16[768,128]{1,0:T(8,128)(2,1)S(1)}, u32[]{:S(2)}, u32[]{:S(2)}) %collective-permute-start.6) | collective-permute-done | bytes 196640 | tf_op jit(solution)/shard_map/ppermute | solution.py:111
  75.8 0.0 collective-permute-done.7.o1_ref
  75.8 0.0 all-to-all-done.2.left_ref
  75.8 3.6 %ladder.1 = f32[8,32,128]{2,1,0:T(8,128)S(1)} custom-call(s32[3]{0:T(128)S(1)} %pad_add_fusion.where_ref, bf16[4,6,256,128]{3,2,1,0:T(8,128)(2,1)} %all-to-all-done.2.left_ref, bf16[768,128]{1,0:T(8,128)(2,1)S(1)} %bitcast.39, bf16[3,768,128]{2,1,0:T(8,128)(2,1)S(1)} %pad_maximum_fusion.r1_ref, bf16[768,128]{1,0:T(8,128)(2,1)S(1)} %collective-permute-done.6.o0_ref, ...), custom_call_target="tpu_custom_call" | custom-call | tf_op jit(solution)/shard_map/ladder/pallas_call | solution.py:116
  79.4 9.6 %all_to_all.25.in_ref = f32[8,32,128]{2,1,0:T(8,128)S(1)} all-to-all(f32[8,32,128]{2,1,0:T(8,128)S(1)} %ladder.1), channel_id=1, replica_groups=mesh['zh'=2,'y'=8,'core'=2,'zl'=6,'x'=4] {'core','x'}, dimensions={0} | all-to-all | bytes 262144 | tf_op jit(solution)/shard_map/all_to_all | solution.py:19
  89.0 0.1 fold.1
  89.1 27.4 %all_to_all.26 = f32[16,4,128]{2,1,0:T(4,128)S(1)} all-to-all(f32[16,4,128]{2,1,0:T(4,128)S(1)} %fold.1), channel_id=1, replica_groups=mesh['zh'=2,'y'=8,'core'=2,'zl'=6,'x'=4] {'zh','y'}, dimensions={0} | all-to-all | bytes 65536 | tf_op jit(solution)/shard_map/all_to_all | solution.py:19
  116.6 0.6 slice_bitcast_fusion
  (5 shorter events, 0.1 us)
Async XLA Ops:
  0.0 1.0 copy-start
  0.0 23.6 %copy-start.1 = (bf16[64,16,512]{2,1,0:T(8,128)(2,1)S(1)}, bf16[64,16,512]{2,1,0:T(8,128)(2,1)}, u32[]{:S(2)}) copy-start(bf16[64,16,512]{2,1,0:T(8,128)(2,1)} %param.5) | copy-start | bytes 3145732
  1.8 9.1 %all-to-all-start = ((bf16[4,32,128]{2,1,0:T(8,128)(2,1)}), bf16[4,32,128]{2,1,0:T(8,128)(2,1)S(1)}, u32[]{:S(2)}, u32[]{:S(2)}) async-start(bf16[4,32,128]{2,1,0:T(8,128)(2,1)} %copy.22), calls=%async_computation | async-start | bytes 65536 | tf_op jit(solution)/shard_map/all_to_all | solution.py:19
  11.8 34.5 %all-to-all-start.1 = ((bf16[6,384,128]{2,1,0:T(8,128)(2,1)}), bf16[6,384,128]{2,1,0:T(8,128)(2,1)S(1)}, u32[]{:S(2)}, u32[]{:S(2)}) async-start(bf16[6,384,128]{2,1,0:T(8,128)(2,1)} %broadcast_in_dim.17), calls=%async_computation.1 | async-start | bytes 1179648 | tf_op jit(solution)/shard_map/all_to_all | solution.py:19
  24.0 22.4 %collective-permute-start = (bf16[16,64,128]{2,1,0:T(8,128)(2,1)S(1)}, bf16[16,64,128]{2,1,0:T(8,128)(2,1)S(1)}, u32[]{:S(2)}, u32[]{:S(2)}) collective-permute-start(bf16[16,64,128]{2,1,0:T(8,128)(2,1)S(1)} %bitcast.42), channel_id=1, source_target_pairs={{0,1},{1,2},{2,3},{3,0},{4,5},{5,6},{6,7},{7,4},{8,9},{9,10},{10,1... | collective-permute-start | bytes 786440 | tf_op jit(solution)/shard_map/ppermute | solution.py:96
  26.2 20.1 %collective-permute-start.1 = (bf16[16,64,128]{2,1,0:T(8,128)(2,1)S(1)}, bf16[16,64,128]{2,1,0:T(8,128)(2,1)S(1)}, u32[]{:S(2)}, u32[]{:S(2)}) collective-permute-start(bf16[16,64,128]{2,1,0:T(8,128)(2,1)S(1)} %bitcast.43), channel_id=1, source_target_pairs={{0,2},{1,3},{2,0},{3,1},{4,6},{5,7},{6,4},{7,5},{8,10},{9,11},{10,... | collective-permute-start | bytes 786440 | tf_op jit(solution)/shard_map/ppermute | solution.py:96
  30.0 16.4 %collective-permute-start.2 = (bf16[16,64,128]{2,1,0:T(8,128)(2,1)S(1)}, bf16[16,64,128]{2,1,0:T(8,128)(2,1)S(1)}, u32[]{:S(2)}, u32[]{:S(2)}) collective-permute-start(bf16[16,64,128]{2,1,0:T(8,128)(2,1)S(1)} %bitcast.44), channel_id=1, source_target_pairs={{0,3},{1,0},{2,1},{3,2},{4,7},{5,4},{6,5},{7,6},{8,11},{9,8},{10,9... | collective-permute-start | bytes 786440 | tf_op jit(solution)/shard_map/ppermute | solution.py:96
  47.9 27.9 %all-to-all-start.2 = ((bf16[4,6,256,128]{3,2,1,0:T(8,128)(2,1)}), bf16[4,6,256,128]{3,2,1,0:T(8,128)(2,1)}, u32[]{:S(2)}, u32[]{:S(2)}) async-start(bf16[4,6,256,128]{3,2,1,0:T(8,128)(2,1)} %broadcast_in_dim.18), calls=%async_computation.2 | async-start | bytes 3145728 | tf_op jit(solution)/shard_map/all_to_all | solution.py:19
  52.2 11.2 %collective-permute-start.5 = (bf16[768,128]{1,0:T(8,128)(2,1)S(1)}, bf16[768,128]{1,0:T(8,128)(2,1)S(1)}, u32[]{:S(2)}, u32[]{:S(2)}) collective-permute-start(bf16[768,128]{1,0:T(8,128)(2,1)S(1)} %bitcast.35), channel_id=1, source_target_pairs={{0,48},{48,96},{96,144},{144,192},{192,240},{240,288},{288,336},{3... | collective-permute-start | bytes 589832 | tf_op jit(solution)/shard_map/ppermute | solution.py:110
  55.4 10.9 %collective-permute-start.4 = (bf16[768,128]{1,0:T(8,128)(2,1)S(1)}, bf16[768,128]{1,0:T(8,128)(2,1)S(1)}, u32[]{:S(2)}, u32[]{:S(2)}) collective-permute-start(bf16[768,128]{1,0:T(8,128)(2,1)S(1)} %bitcast.36), channel_id=1, source_target_pairs={{0,96},{48,336},{96,192},{144,48},{192,288},{240,144},{288,0},{336... | collective-permute-start | bytes 589832 | tf_op jit(solution)/shard_map/ppermute | solution.py:110
  59.7 8.9 %collective-permute-start.3 = (bf16[768,128]{1,0:T(8,128)(2,1)S(1)}, bf16[768,128]{1,0:T(8,128)(2,1)S(1)}, u32[]{:S(2)}, u32[]{:S(2)}) collective-permute-start(bf16[768,128]{1,0:T(8,128)(2,1)S(1)} %bitcast.37), channel_id=1, source_target_pairs={{0,336},{48,0},{96,48},{144,96},{192,144},{240,192},{288,240},{336... | collective-permute-start | bytes 589832 | tf_op jit(solution)/shard_map/ppermute | solution.py:110
  68.6 7.2 %collective-permute-start.7 = (bf16[3,768,128]{2,1,0:T(8,128)(2,1)S(1)}, bf16[3,768,128]{2,1,0:T(8,128)(2,1)S(1)}, u32[]{:S(2)}, u32[]{:S(2)}) collective-permute-start(bf16[3,768,128]{2,1,0:T(8,128)(2,1)S(1)} %pad_maximum_fusion.r1_ref), channel_id=1, source_target_pairs={{0,24},{24,0},{1,25},{25,1},{2,26},{26,2},{3,27},{27,3},{4,28},{28... | collective-permute-start | bytes 1769480 | tf_op jit(solution)/shard_map/ppermute | solution.py:113
  72.5 3.3 %collective-permute-start.6 = (bf16[768,128]{1,0:T(8,128)(2,1)S(1)}, bf16[768,128]{1,0:T(8,128)(2,1)S(1)}, u32[]{:S(2)}, u32[]{:S(2)}) collective-permute-start(bf16[768,128]{1,0:T(8,128)(2,1)S(1)} %bitcast.38), channel_id=1, source_target_pairs={{0,24},{24,0},{1,25},{25,1},{2,26},{26,2},{3,27},{27,3},{4,28},{28... | collective-permute-start | bytes 589832 | tf_op jit(solution)/shard_map/ppermute | solution.py:111
